TPU v7x, 512 devices: a whole 4x8x8 slice. The times are simulated.
512 devices in a mesh: dp: 64 (over z_hi, y, x), blk: 8 (over z_lo, core).
Axes of the slice: x: 4, y: 8, z: 8 (z_hi: 2, z_lo: 4; z = z_hi * 4 + z_lo), core: 2. Of those that a mesh axis runs over, the one named last changes fastest.
Arguments:
- train_act: bfloat16 [2048, 4096], P(('dp', 'blk')), may hold values from -3 to 3
- train_grad: bfloat16 [2048, 8192], P(('dp', 'blk')), may hold values from -3 to 3
- query_act: bfloat16 [256, 4096], P('dp', 'blk'), may hold values from -3 to 3
- query_grad: bfloat16 [256, 8192], P('dp'), may hold values from -3 to 3
- act_basis: bfloat16 [4096, 512], P('blk'), may hold values from -0.25 to 0.25
- grad_basis: bfloat16 [512, 8192], P(None, 'dp'), may hold values from -0.25 to 0.25
- eigenvalues: float32 [4096, 8192], P('blk', 'dp'), may hold values from 0.05 to 5
- example_ids: int32 [2048], replicated, may hold values from 0 to 127, never falling along the last dimension, each value on 1 to 48 neighbouring positions
- query_ids: int32 [256], replicated, may hold values from 0 to 15, never falling along the last dimension, each value on 1 to 48 neighbouring positions
Outputs:
- influence: float32 [128, 16], P('dp')
Inputs may be any that keep to these rules, and one draw needn't show every extreme that they name: `example_ids`: the tokens of one training example are contiguous and ids never fall; every example has a token. `query_ids`: the tokens of one query are contiguous and ids never fall; every query has a token.
All inputs are finite; a program needn't handle non-finite values.
Results may differ from a plain program's by a relative error of at most 0.0007.
The roundings to bfloat16 on the way count: a program that leaves them out, or rounds other values in their place, can miss the bound.
Values may be sent and summed in bfloat16 or wider, within the bound.
No kernel may reach another device: no remote copies, remote signals or barrier semaphores. Data moves between devices by JAX's collectives and lax.ppermute only.
A program may use at most 64 MiB of HBM per device.

v0:
```python
import jax
import jax.numpy as jnp
from jax import lax
from jax.sharding import PartitionSpec as P

D = 4096
FF = 8192
QUERIES = 16
EX_DP = 2


def partner(block, axis, stride):
    count = lax.axis_size(axis)
    route = []
    for low in range(count):
        high = low | 1 << stride
        if high != low and high < count:
            route += [(low, high), (high, low)]
    return lax.ppermute(block, axis, route)


def rotate_blocks(row_data, basis):
    row_count = row_data.shape[0]
    block_size = basis.shape[1]
    count_blocks = basis.shape[0] // block_size
    turned = jnp.einsum(
        "tnk,nkl->tnl",
        row_data.reshape(row_count, count_blocks, block_size),
        basis.reshape(count_blocks, block_size, block_size),
        preferred_element_type=jnp.float32,
    )
    return turned.reshape(row_count, count_blocks * block_size).astype(jnp.bfloat16)


def rotate_columns(row_data, basis):
    row_count = row_data.shape[0]
    full_width = row_data.shape[1]
    block_size = basis.shape[0]
    col_width = basis.shape[1]
    count_blocks = full_width // block_size
    turned = jnp.einsum(
        "tmk,kml->tml",
        row_data.reshape(row_count, count_blocks, block_size),
        basis.reshape(block_size, count_blocks, col_width // count_blocks),
        preferred_element_type=jnp.float32,
    )
    return turned.reshape(row_count, col_width).astype(jnp.bfloat16)


def join_pair(mine, other, is_upper):
    return jnp.where(is_upper, jnp.concatenate([other, mine], 1), jnp.concatenate([mine, other], 1))


def shards(
    train_act,
    train_grad,
    query_act,
    query_grad,
    act_basis,
    grad_basis,
    eigenvalues,
    example_ids,
    query_ids,
):
    devices_dp = lax.axis_size("dp")
    block_size = grad_basis.shape[0]
    col_width = grad_basis.shape[1]
    owned_width = act_basis.shape[0]
    eigen_sum = lax.psum(jnp.sum(eigenvalues), ("dp", "blk"))
    damping = 0.1 * eigen_sum / (D * FF)
    owned_rows = lax.all_to_all(train_act, "blk", split_axis=1, concat_axis=0, tiled=True)
    query_all = lax.all_gather(rotate_blocks(query_act, act_basis), "dp", axis=0, tiled=True)
    train_cols, query_cols = (
        lax.all_to_all(train_grad, "dp", split_axis=1, concat_axis=0, tiled=True),
        lax.all_to_all(query_grad, "dp", split_axis=1, concat_axis=0, tiled=True),
    )
    position = lax.axis_index("dp")
    for bit_index in range((block_size // col_width).bit_length() - 1):
        other_train, other_query = partner((train_cols, query_cols), "dp", bit_index)
        is_upper = position >> bit_index & 1 == 1
        train_cols = join_pair(train_cols, other_train, is_upper)
        query_cols = join_pair(query_cols, other_query, is_upper)
    grad_mine = rotate_columns(train_cols, grad_basis)
    query_grad_rot = rotate_columns(query_cols, grad_basis)
    grad_all = lax.all_gather(
        grad_mine.reshape(devices_dp, 1, grad_mine.shape[0] // devices_dp, col_width),
        "blk",
        axis=1,
        tiled=True,
    )
    grad_all = grad_all.reshape(
        grad_all.shape[0] * grad_all.shape[1] * grad_all.shape[2], col_width
    )
    one_query = (query_ids[:, None] == jnp.arange(QUERIES, dtype=jnp.int32)[None, :]).astype(
        jnp.bfloat16
    )
    weighted = one_query.T[:, :, None] * query_all[None, :, :]
    query_gram = jnp.einsum(
        "qti,tj->iqj", weighted, query_grad_rot, preferred_element_type=jnp.float32
    )
    norm_scale = float(D * FF) ** (-0.5)
    precond = (query_gram / (eigenvalues[:, None, :] + damping) * norm_scale).astype(jnp.bfloat16)
    precond = precond.reshape(owned_width, QUERIES * col_width)
    shard_rows = lax.all_gather(rotate_blocks(owned_rows, act_basis), "dp", axis=0, tiled=True)
    row_count = shard_rows.shape[0]
    mixed_rows = jnp.dot(shard_rows, precond, preferred_element_type=jnp.float32).reshape(
        row_count, QUERIES, col_width
    )
    token_score = jnp.sum(mixed_rows * grad_all[:, None, :].astype(jnp.float32), axis=2)
    example_count = EX_DP * devices_dp
    one_example = (
        example_ids[:, None] == jnp.arange(example_count, dtype=jnp.int32)[None, :]
    ).astype(jnp.float32)
    partial_scores = jnp.dot(one_example.T, token_score, precision=lax.Precision.HIGHEST)
    all_scores = lax.psum(partial_scores, ("dp", "blk"))
    return lax.dynamic_slice_in_dim(all_scores, lax.axis_index("dp") * EX_DP, EX_DP, 0)


def solution(mesh):
    placed = (
        P(("dp", "blk"), None),
        P(("dp", "blk"), None),
        P("dp", "blk"),
        P("dp", None),
        P("blk", None),
        P(None, "dp"),
        P("blk", "dp"),
        P(),
        P(),
    )
    return jax.shard_map(
        shards, mesh=mesh, in_specs=placed, out_specs=P("dp", None), check_vma=False
    )
```

profile of v0, /device:TPU:1, one launch (start us, length us, event | category | flops | bytes accessed | tf_op | source)
XLA Modules:
  0.0 528.6 jit_solution(4616958831097814002)
XLA Ops:
  6.5 0.0 copy-start
  6.5 15.2 %all_to_all.54 = bf16[4,8,512]{2,0,1:T(4,128)(2,1)S(1)} all-to-all(bf16[4,8,512]{2,0,1:T(4,128)(2,1)} %bitcast.73), channel_id=1, replica_groups=mesh['dp'=64,'blk'=8] {'blk'}, dimensions={1} | all-to-all | bytes 65536 | tf_op jit(solution)/shard_map/all_to_all | solution.py:71
  21.8 0.0 copy-done
  21.8 0.8 fusion.10
  22.6 0.0 all-gather.4.cloned.1.call-update
  22.6 1.6 reduce_sum.18
  24.2 14.7 %all-to-all-start.2 = ((bf16[4,64,128]{2,0,1:T(4,128)(2,1)}), bf16[4,64,128]{2,0,1:T(4,128)(2,1)S(1)}, u32[]{:S(2)}, u32[]{:S(2)}) async-start(bf16[4,64,128]{2,0,1:T(4,128)(2,1)} %bitcast.71), calls=%async_computation.2 | async-start | bytes 131072 | tf_op jit(solution)/shard_map/all_to_all | solution.py:74
  38.9 104.2 %psum.14 = f32[]{:T(128)} all-reduce(f32[]{:T(128)} %reduce_sum.18), channel_id=1, replica_groups=mesh['dp'=64,'blk'=8] {'dp','blk'}, use_global_device_ids=true, to_apply=%region_1.0 | all-reduce | flops 1 | bytes 8 | tf_op jit(solution)/shard_map/psum | solution.py:69
  143.7 1.0 broadcast_add_fusion
  144.7 0.7 fusion.34
  145.4 0.0 all-to-all-done.2
  145.4 10.7 %all-to-all-start.1 = ((bf16[4,64,128]{2,0,1:T(4,128)(2,1)}), bf16[4,64,128]{2,0,1:T(4,128)(2,1)S(1)}, u32[]{:S(2)}, u32[]{:S(2)}) async-start(bf16[4,64,128]{2,0,1:T(4,128)(2,1)} %bitcast.72), calls=%async_computation.1 | async-start | bytes 131072 | tf_op jit(solution)/shard_map/all_to_all | solution.py:75
  156.1 2.9 collective-permute-start.2
  159.0 0.9 fusion.11
  159.9 9.7 %all-to-all-done.1 = bf16[4,64,128]{2,0,1:T(4,128)(2,1)S(1)} async-done(((bf16[4,64,128]{2,0,1:T(4,128)(2,1)}), bf16[4,64,128]{2,0,1:T(4,128)(2,1)S(1)}, u32[]{:S(2)}, u32[]{:S(2)}) %all-to-all-start.1) | async-done | bytes 65568 | tf_op jit(solution)/shard_map/all_to_all | solution.py:75
  169.6 2.2 collective-permute-start
  171.8 0.0 collective-permute-done.2
  171.9 3.9 collective-permute-start.3
  175.9 189.5 %all-gather.1 = bf16[256,1,512]{2,1,0:T(2,128)(2,1)S(1)} all-gather(bf16[4,1,512]{2,1,0:T(2,128)(2,1)S(1)} %copy.34), channel_id=3, replica_groups=mesh['dp'=64,'blk'=8] {'dp'}, dimensions={0}, use_global_device_ids=true | all-gather | bytes 266240 | tf_op jit(solution)/shard_map/all_gather | solution.py:72
  365.3 0.1 copy.36
  365.5 0.0 collective-permute-done
  365.5 1.9 collective-permute-start.1
  367.5 0.0 collective-permute-done.3
  367.5 0.2 convolution_convert_fusion
  367.7 45.3 %all_gather.11 = bf16[64,8,4,128]{3,2,1,0:T(4,128)(2,1)S(1)} all-gather(bf16[64,1,4,128]{3,2,1,0:T(4,128)(2,1)S(1)} %bitcast.70), channel_id=1, replica_groups=mesh['dp'=64,'blk'=8] {'blk'}, dimensions={1}, use_global_device_ids=true | all-gather | bytes 589824 | tf_op jit(solution)/shard_map/all_gather | solution.py:85
  413.0 0.2 copy.39
  413.3 0.0 collective-permute-done.1
  413.3 3.0 fusion.2
  416.2 7.7 %multiply_reduce_fusion = f32[2048,16]{0,1:T(8,128)S(1)} fusion(f32[2048,128]{0,1:T(8,128)S(1)} %copy.39, bf16[2048,1,512]{2,0,1:T(8,128)(2,1)} %all-gather.4.cloned.1.call-done, f32[128,16,512]{2,0,1:T(8,128)} %fusion.2, f32[512,128]{0,1:T(8,128)S(1)} %copy.36), kind=kOutput, calls=%fused_computation | convolution fusion | flops 4306468864 | bytes 7733248 | tf_op jit(solution)/shard_map/dot_general | solution.py:106
  424.0 1.1 fusion.13
  425.1 96.1 %psum.15 = f32[128,16]{1,0:T(8,128)S(1)} all-reduce(f32[128,16]{1,0:T(8,128)S(1)} %fusion.13), channel_id=1, replica_groups=mesh['dp'=64,'blk'=8] {'dp','blk'}, use_global_device_ids=true, to_apply=%region_3.4 | all-reduce | flops 2048 | bytes 16384 | tf_op jit(solution)/shard_map/psum | solution.py:115
  521.1 0.6 constant_dynamic-slice_fusion
  (11 shorter events, 0.2 us)
Async XLA Ops:
  6.5 15.2 %copy-start = (bf16[512,512]{1,0:T(8,128)(2,1)S(1)}, bf16[512,512]{1,0:T(8,128)(2,1)}, u32[]{:S(2)}) copy-start(bf16[512,512]{1,0:T(8,128)(2,1)} %param.13) | copy-start | bytes 1572868
  6.5 360.9 %copy-start.1 = (bf16[512,128]{1,0:T(8,128)(2,1)S(1)}, bf16[512,128]{1,0:T(8,128)(2,1)}, u32[]{:S(2)}) copy-start(bf16[512,128]{1,0:T(8,128)(2,1)} %param.14) | copy-start | bytes 393220
  6.5 409.7 %all-gather.4.cloned.1.call-start = ((), (), s32[]{:S(2)}) async-start(), calls=%async_computation.3 | async-start | bytes 2129920 | tf_op jit(solution)/shard_map/all_gather | solution.py:104
  24.2 121.2 %all-to-all-start.2 = ((bf16[4,64,128]{2,0,1:T(4,128)(2,1)}), bf16[4,64,128]{2,0,1:T(4,128)(2,1)S(1)}, u32[]{:S(2)}, u32[]{:S(2)}) async-start(bf16[4,64,128]{2,0,1:T(4,128)(2,1)} %bitcast.71), calls=%async_computation.2 | async-start | bytes 131072 | tf_op jit(solution)/shard_map/all_to_all | solution.py:74
  145.4 24.2 %all-to-all-start.1 = ((bf16[4,64,128]{2,0,1:T(4,128)(2,1)}), bf16[4,64,128]{2,0,1:T(4,128)(2,1)S(1)}, u32[]{:S(2)}, u32[]{:S(2)}) async-start(bf16[4,64,128]{2,0,1:T(4,128)(2,1)} %bitcast.72), calls=%async_computation.1 | async-start | bytes 131072 | tf_op jit(solution)/shard_map/all_to_all | solution.py:75
  156.1 15.7 %collective-permute-start.2 = (bf16[256,128]{1,0:T(8,128)(2,1)S(1)}, bf16[256,128]{1,0:T(8,128)(2,1)S(1)}, u32[]{:S(2)}, u32[]{:S(2)}) collective-permute-start(bf16[256,128]{1,0:T(8,128)(2,1)S(1)} %bitcast.67), channel_id=1, source_target_pairs={{0,8},{8,0},{16,24},{24,16},{32,40},{40,32},{48,56},{56,48},{64,72... | collective-permute-start | bytes 196616 | tf_op jit(solution)/shard_map/ppermute | solution.py:19
  169.6 195.8 %collective-permute-start = (bf16[256,128]{1,0:T(8,128)(2,1)S(1)}, bf16[256,128]{1,0:T(8,128)(2,1)S(1)}, u32[]{:S(2)}, u32[]{:S(2)}) collective-permute-start(bf16[256,128]{1,0:T(8,128)(2,1)S(1)} %bitcast.65), channel_id=1, source_target_pairs={{0,8},{8,0},{16,24},{24,16},{32,40},{40,32},{48,56},{56,48},{64,72... | collective-permute-start | bytes 196616 | tf_op jit(solution)/shard_map/ppermute | solution.py:19
  171.9 195.6 %collective-permute-start.3 = (bf16[256,256]{1,0:T(8,128)(2,1)S(1)}, bf16[256,256]{1,0:T(8,128)(2,1)S(1)}, u32[]{:S(2)}, u32[]{:S(2)}) collective-permute-start(bf16[256,256]{1,0:T(8,128)(2,1)S(1)} %maximum_select_fusion.6), channel_id=1, source_target_pairs={{0,16},{16,0},{8,24},{24,8},{32,48},{48,32},{40,56},{56,40},{64,80... | collective-permute-start | bytes 393224 | tf_op jit(solution)/shard_map/ppermute | solution.py:19
  365.5 47.7 %collective-permute-start.1 = (bf16[256,256]{1,0:T(8,128)(2,1)S(1)}, bf16[256,256]{1,0:T(8,128)(2,1)S(1)}, u32[]{:S(2)}, u32[]{:S(2)}) collective-permute-start(bf16[256,256]{1,0:T(8,128)(2,1)S(1)} %maximum_select_fusion.5), channel_id=1, source_target_pairs={{0,16},{16,0},{8,24},{24,8},{32,48},{48,32},{40,56},{56,40},{64,80... | collective-permute-start | bytes 393224 | tf_op jit(solution)/shard_map/ppermute | solution.py:19
  416.2 7.7 %copy-start.2 = (s32[2048]{0:T(1024)S(1)}, s32[2048]{0:T(1024)}, u32[]{:S(2)}) copy-start(s32[2048]{0:T(1024)} %param.16) | copy-start | bytes 24580
Sparse Core Ops, SparseCore 0:
  22.7 136.6 all-gather.3
where the time goes:
time: 529 us
  blocking collectives  450 us (85%)
  starting transfers between devices  36.4 us (7%)
  between operations  14.2 us (3%)
  matrix products  13.6 us (3%)
  waiting for transfers between devices  9.75 us (2%)
    all_gather x1, blocking collectives, shards(): lax.all_gather(rotate_blocks(query_act, act_basis), 'dp', axis=0, tiled=T...  189 us
    psum x1, blocking collectives, shards(): eigen_sum = lax.psum(jnp.sum(eigenvalues), ('dp', 'blk'))  104 us
    psum x1, blocking collectives, shards(): all_scores = lax.psum(partial_scores, ('dp', 'blk'))  96.1 us
    all_gather x1, blocking collectives, shards(): lax.all_gather(grad_mine.reshape(devices_dp, 1, grad_mine.shape[0] // dev...  45.3 us
    all_to_all x1, blocking collectives, shards(): lax.all_to_all(train_act, 'blk', split_axis=1, concat_axis=0, tiled=True)  15.2 us
    all_to_all x1, starting transfers between devices, shards(): lax.all_to_all(train_grad, 'dp', split_axis=1, concat_axis=0, tiled=True)  14.7 us
    ppermute x4, starting transfers between devices, partner(): return lax.ppermute(block, axis, route)  11 us
    all_to_all x1, starting transfers between devices, shards(): lax.all_to_all(query_grad, 'dp', split_axis=1, concat_axis=0, tiled=True)  10.7 us
  transfers between devices with their start and end apart: 7, of which 1 were waited for; matrix products, arithmetic and copies ran while one was open for 1% of the time, Pallas kernels for 0%

commit v1 on v0

--- a/solution.py
+++ b/solution.py
@@ -7,6 +7,7 @@
 FF = 8192
 QUERIES = 16
 EX_DP = 2
+_meet_block = lambda axis_id, shard_in: jnp.sum(lax.all_gather(shard_in, axis_id), axis=0)
 
 
 def partner(block, axis, stride):
@@ -112,7 +113,7 @@
         example_ids[:, None] == jnp.arange(example_count, dtype=jnp.int32)[None, :]
     ).astype(jnp.float32)
     partial_scores = jnp.dot(one_example.T, token_score, precision=lax.Precision.HIGHEST)
-    all_scores = lax.psum(partial_scores, ("dp", "blk"))
+    all_scores = _meet_block(("dp", "blk"), partial_scores)
     return lax.dynamic_slice_in_dim(all_scores, lax.axis_index("dp") * EX_DP, EX_DP, 0)
 
 

time: 529 us -> 1200 us (2.27)
  waiting for transfers between devices: 9.75 us -> 777 us
  blocking collectives: 450 us -> 354 us
    all_gather x0 -> x1, waiting for transfers between devices: none -> 767 us  [lax.all_gather(shard_in, axis_id)]
    psum x1 -> x0, blocking collectives: 96.1 us -> none  [shards(): all_scores = lax.psum(partial_scores, ('dp', 'blk'))]
  transfers between devices with their start and end apart: 7 -> 8, of which waited for: 1 -> 2; matrix products, arithmetic and copies ran while one was open for 1% -> 1% of each run, Pallas kernels for 0% -> 0%
where the time goes in v1:
time: 1200 us
  waiting for transfers between devices  777 us (65%)
  blocking collectives  354 us (30%)
  starting transfers between devices  36.4 us (3%)
  between operations  14.2 us (1%)
  matrix products  13.5 us (1%)
    all_gather x1, waiting for transfers between devices, lax.all_gather(shard_in, axis_id)  767 us
    all_gather x1, blocking collectives, shards(): lax.all_gather(rotate_blocks(query_act, act_basis), 'dp', axis=0, tiled=T...  189 us
    psum x1, blocking collectives, shards(): eigen_sum = lax.psum(jnp.sum(eigenvalues), ('dp', 'blk'))  104 us
    all_gather x1, blocking collectives, shards(): lax.all_gather(grad_mine.reshape(devices_dp, 1, grad_mine.shape[0] // dev...  45.8 us
  transfers between devices with their start and end apart: 8, of which 2 were waited for; matrix products, arithmetic and copies ran while one was open for 1% of the time, Pallas kernels for 0%

profile of v1, /device:TPU:1, one launch (start us, length us, event | category | flops | bytes accessed | tf_op | source)
XLA Modules:
  0.0 1203.1 jit_solution(15559847975174981257)
XLA Ops:
  6.5 15.2 %all_to_all.54 = bf16[4,8,512]{2,0,1:T(4,128)(2,1)S(1)} all-to-all(bf16[4,8,512]{2,0,1:T(4,128)(2,1)} %bitcast.79), channel_id=1, replica_groups=mesh['dp'=64,'blk'=8] {'blk'}, dimensions={1} | all-to-all | bytes 65536 | tf_op jit(solution)/shard_map/all_to_all | solution.py:72
  21.8 0.8 fusion.10
  22.6 0.0 all-gather.6.cloned.1.call-update
  22.6 1.6 reduce_sum.27
  24.2 14.7 %all-to-all-start.2 = ((bf16[4,64,128]{2,0,1:T(4,128)(2,1)}), bf16[4,64,128]{2,0,1:T(4,128)(2,1)S(1)}, u32[]{:S(2)}, u32[]{:S(2)}) async-start(bf16[4,64,128]{2,0,1:T(4,128)(2,1)} %bitcast.77), calls=%async_computation.2 | async-start | bytes 131072 | tf_op jit(solution)/shard_map/all_to_all | solution.py:75
  38.9 104.2 %psum.7 = f32[]{:T(128)} all-reduce(f32[]{:T(128)} %reduce_sum.27), channel_id=1, replica_groups=mesh['dp'=64,'blk'=8] {'dp','blk'}, use_global_device_ids=true, to_apply=%region_1.0 | all-reduce | flops 1 | bytes 8 | tf_op jit(solution)/shard_map/psum | solution.py:70
  143.7 1.0 broadcast_add_fusion
  144.7 0.7 fusion.32
  145.4 10.6 all-to-all-start.1
  156.1 0.0 all-gather.8.cloned.1.call-start
  156.1 2.9 collective-permute-start.2
  159.0 0.9 fusion.11
  159.9 9.7 all-to-all-done.1
  169.6 2.2 collective-permute-start
  171.8 0.0 collective-permute-done.2
  171.8 4.0 collective-permute-start.3
  175.8 189.0 %all-gather.1 = bf16[256,1,512]{2,1,0:T(2,128)(2,1)S(1)} all-gather(bf16[4,1,512]{2,1,0:T(2,128)(2,1)S(1)} %copy.36), channel_id=3, replica_groups=mesh['dp'=64,'blk'=8] {'dp'}, dimensions={0}, use_global_device_ids=true | all-gather | bytes 266240 | tf_op jit(solution)/shard_map/all_gather | solution.py:73
  364.8 0.1 copy.38
  365.0 1.9 collective-permute-start.1
  367.0 0.2 convolution_convert_fusion
  367.2 45.8 %all_gather.17 = bf16[64,8,4,128]{3,2,1,0:T(4,128)(2,1)S(1)} all-gather(bf16[64,1,4,128]{3,2,1,0:T(4,128)(2,1)S(1)} %bitcast.76), channel_id=1, replica_groups=mesh['dp'=64,'blk'=8] {'blk'}, dimensions={1}, use_global_device_ids=true | all-gather | bytes 589824 | tf_op jit(solution)/shard_map/all_gather | solution.py:86
  413.0 0.2 copy.41
  413.2 0.0 collective-permute-done.1
  413.3 3.0 fusion.2
  416.2 7.5 multiply_reduce_fusion
  423.7 1.2 fusion.12
  424.9 0.0 all-gather.8.cloned.1.call-update
  425.0 767.3 %all-gather.8.cloned.1.call-done = f32[65536,16]{0,1:T(8,128)} async-done(((f32[128,16]{0,1:T(8,128)}), f32[65536,16]{0,1:T(8,128)}) %all-gather.8.cloned.1.call-update) | async-done | bytes 4194320 | tf_op jit(solution)/shard_map/all_gather | solution.py:10
  1192.3 3.0 copy.46
  1195.3 0.2 bitcast_reduce_fusion
  1195.5 0.1 constant_dynamic-slice_fusion
  1195.6 0.6 copy.42
  (16 shorter events, 0.2 us)
Async XLA Ops:
  6.5 15.2 %copy-start = (bf16[512,512]{1,0:T(8,128)(2,1)S(1)}, bf16[512,512]{1,0:T(8,128)(2,1)}, u32[]{:S(2)}) copy-start(bf16[512,512]{1,0:T(8,128)(2,1)} %param.13) | copy-start | bytes 1572868
  6.5 360.4 %copy-start.1 = (bf16[512,128]{1,0:T(8,128)(2,1)S(1)}, bf16[512,128]{1,0:T(8,128)(2,1)}, u32[]{:S(2)}) copy-start(bf16[512,128]{1,0:T(8,128)(2,1)} %param.14) | copy-start | bytes 393220
  6.5 409.7 %all-gather.6.cloned.1.call-start = ((), (), s32[]{:S(2)}) async-start(), calls=%async_computation.3 | async-start | bytes 2129920 | tf_op jit(solution)/shard_map/all_gather | solution.py:105
  24.2 121.2 %all-to-all-start.2 = ((bf16[4,64,128]{2,0,1:T(4,128)(2,1)}), bf16[4,64,128]{2,0,1:T(4,128)(2,1)S(1)}, u32[]{:S(2)}, u32[]{:S(2)}) async-start(bf16[4,64,128]{2,0,1:T(4,128)(2,1)} %bitcast.77), calls=%async_computation.2 | async-start | bytes 131072 | tf_op jit(solution)/shard_map/all_to_all | solution.py:75
  145.4 24.2 %all-to-all-start.1 = ((bf16[4,64,128]{2,0,1:T(4,128)(2,1)}), bf16[4,64,128]{2,0,1:T(4,128)(2,1)S(1)}, u32[]{:S(2)}, u32[]{:S(2)}) async-start(bf16[4,64,128]{2,0,1:T(4,128)(2,1)} %bitcast.78), calls=%async_computation.1 | async-start | bytes 131072 | tf_op jit(solution)/shard_map/all_to_all | solution.py:76
  156.1 1036.2 %all-gather.8.cloned.1.call-start = ((), (), s32[]{:S(2)}) async-start(), calls=%async_computation.4 | async-start | bytes 4202496 | tf_op jit(solution)/shard_map/all_gather | solution.py:10
  156.1 15.7 %collective-permute-start.2 = (bf16[256,128]{1,0:T(8,128)(2,1)S(1)}, bf16[256,128]{1,0:T(8,128)(2,1)S(1)}, u32[]{:S(2)}, u32[]{:S(2)}) collective-permute-start(bf16[256,128]{1,0:T(8,128)(2,1)S(1)} %bitcast.73), channel_id=1, source_target_pairs={{0,8},{8,0},{16,24},{24,16},{32,40},{40,32},{48,56},{56,48},{64,72... | collective-permute-start | bytes 196616 | tf_op jit(solution)/shard_map/ppermute | solution.py:20
  169.6 195.4 %collective-permute-start = (bf16[256,128]{1,0:T(8,128)(2,1)S(1)}, bf16[256,128]{1,0:T(8,128)(2,1)S(1)}, u32[]{:S(2)}, u32[]{:S(2)}) collective-permute-start(bf16[256,128]{1,0:T(8,128)(2,1)S(1)} %bitcast.71), channel_id=1, source_target_pairs={{0,8},{8,0},{16,24},{24,16},{32,40},{40,32},{48,56},{56,48},{64,72... | collective-permute-start | bytes 196616 | tf_op jit(solution)/shard_map/ppermute | solution.py:20
  171.8 195.1 %collective-permute-start.3 = (bf16[256,256]{1,0:T(8,128)(2,1)S(1)}, bf16[256,256]{1,0:T(8,128)(2,1)S(1)}, u32[]{:S(2)}, u32[]{:S(2)}) collective-permute-start(bf16[256,256]{1,0:T(8,128)(2,1)S(1)} %maximum_select_fusion.6), channel_id=1, source_target_pairs={{0,16},{16,0},{8,24},{24,8},{32,48},{48,32},{40,56},{56,40},{64,80... | collective-permute-start | bytes 393224 | tf_op jit(solution)/shard_map/ppermute | solution.py:20
  365.0 48.2 %collective-permute-start.1 = (bf16[256,256]{1,0:T(8,128)(2,1)S(1)}, bf16[256,256]{1,0:T(8,128)(2,1)S(1)}, u32[]{:S(2)}, u32[]{:S(2)}) collective-permute-start(bf16[256,256]{1,0:T(8,128)(2,1)S(1)} %maximum_select_fusion.5), channel_id=1, source_target_pairs={{0,16},{16,0},{8,24},{24,8},{32,48},{48,32},{40,56},{56,40},{64,80... | collective-permute-start | bytes 393224 | tf_op jit(solution)/shard_map/ppermute | solution.py:20
  416.2 7.5 copy-start.2
Sparse Core Ops, SparseCore 0:
  22.7 136.6 all-gather.5
  425.1 767.1 all-gather.7
